TPU v7x, 32 devices: a whole 2x2x4 slice. The times are simulated.
32 devices in a mesh: theta: 16 (over z, x, core), xr: 2 (over y).
Axes of the slice: x: 2, y: 2, z: 4, core: 2. Of those that a mesh axis runs over, the one named last changes fastest.
Arguments:
- state: float32 [3, 2, 5, 128, 16, 128], P(None, None, None, 'theta', 'xr'), may hold values from -6 to 6
- source: float32 [3, 2, 5, 128, 16, 128], P(None, None, None, 'theta', 'xr'), may hold values from -6 to 6
- sigma: float32 [128, 16, 128], P('theta', 'xr'), may hold values from 0.25 to 4
- stagger: int32 [32], P('theta'), may hold values from 0 to 3
- a_theta: float32 [4, 5, 5], replicated, may hold values from -2.5 to 2.5
- a_axial: float32 [5, 5], replicated, may hold values from -2.5 to 2.5
- a_radial: float32 [5, 5], replicated, may hold values from -2.5 to 2.5
- mode_order: int32 [3, 128], replicated, may hold values from -32 to 32
- mode_radial: int32 [3, 128], replicated, may hold values from 0 to 7
- mode_plane: int32 [3, 128], replicated, may hold values from 0 to 1
- gust: float32 [3, 2, 128], replicated, may hold values from -6 to 6
- l_rows: float32 [2, 5], replicated, may hold values from -4 to 4
- r_cols: float32 [2, 5], replicated, may hold values from -4 to 4
Outputs:
- fields: float32 [3, 2, 5, 128, 16, 128], P(None, None, None, 'theta', 'xr')
- amplitudes: float32 [3, 2, 2, 128], replicated
Inputs may be any that keep to these rules, and one draw needn't show every extreme that they name: `mode_plane`: 0 names the inlet plane, 1 the exit plane.
All inputs are finite; a program needn't handle non-finite values.
Results may differ from a plain program's by a relative error of at most 0.0003.
Values sent between devices are 32-bit elements; how exact they have to be, the bound alone decides.
A program may use at most 64 MiB of HBM per device.

v0:
```python
import math

import jax
import jax.numpy as jnp
from jax import lax
from jax.sharding import PartitionSpec as P

courant = 0.5
viscosity = 0.1
base_frequency = 0.5
highest = lax.Precision.HIGHEST


def extended(array, sides, width, wrap):
    for axis, dim in sides:
        devices, length = (lax.axis_size(axis), array.shape[dim])
        up = [(i, (i + 1) % devices) for i in range(devices if wrap else devices - 1)]
        down = [(j, i) for i, j in up]
        last = lax.slice_in_dim(array, length - width, length, axis=dim)
        initial = lax.slice_in_dim(array, 0, width, axis=dim)
        before = lax.ppermute(last, axis, up)
        after = lax.ppermute(initial, axis, down)
        array = jnp.concatenate([before, array, after], axis=dim)
    return array


def local_residual(
    field, theta_ext, axial_ext, freqs, forcing, damping, passage_matrix, a_axial, a_radial
):
    nharm, two, nvar, ctheta, caxial, nradial = field.shape
    npass = passage_matrix.shape[0]
    diff_theta = (theta_ext[:, :, :, 2:] - theta_ext[:, :, :, :-2]) * 0.5
    lap_theta = theta_ext[:, :, :, 2:] + theta_ext[:, :, :, :-2] - 2.0 * field
    diff_axial = (axial_ext[:, :, :, :, 2:] - axial_ext[:, :, :, :, :-2]) * 0.5
    lap_axial = axial_ext[:, :, :, :, 2:] + axial_ext[:, :, :, :, :-2] - 2.0 * field
    padded = jnp.pad(field, ((0, 0), (0, 0), (0, 0), (0, 0), (0, 0), (1, 1)))
    diff_radial = (padded[..., 2:] - padded[..., :-2]) * 0.5
    lap_radial = padded[..., 2:] + padded[..., :-2] - 2.0 * field
    turned = jnp.stack([-field[:, 1], field[:, 0]], axis=1)
    grouped = diff_theta.reshape(nharm, two, nvar, npass, ctheta // npass, caxial, nradial)
    flux = jnp.einsum("kvw,hpwkcxr->hpvkcxr", passage_matrix, grouped, precision=highest).reshape(
        field.shape
    )
    flux = flux + jnp.einsum("vw,hpwtxr->hpvtxr", a_axial, diff_axial, precision=highest)
    flux = flux + jnp.einsum("vw,hpwtxr->hpvtxr", a_radial, diff_radial, precision=highest)
    return (
        freqs[:, None, None, None, None, None] * turned
        + flux
        - viscosity * (lap_theta + lap_axial + lap_radial)
        + damping * field
        - forcing
    )


def local(
    state,
    source,
    sigma,
    stagger,
    a_theta,
    a_axial,
    a_radial,
    mode_order,
    mode_radial,
    mode_plane,
    gust,
    l_rows,
    r_cols,
):
    nharm, two, nvar, ctheta, caxial, nradial = state.shape
    total_theta = ctheta * lax.axis_size("theta")
    scale = 1.0 / math.sqrt(total_theta * nradial)
    freqs = base_frequency * (1.0 + jnp.arange(nharm).astype(jnp.float32))
    onehot = (stagger[:, None] == jnp.arange(a_theta.shape[0])[None, :]).astype(jnp.float32)
    passage_matrix = jnp.einsum("ks,svw->kvw", onehot, a_theta, precision=highest)
    step_size = courant / (1.0 + sigma)
    xr_index = lax.axis_index("xr")
    is_first = (xr_index == 0).astype(jnp.float32)
    is_last = (xr_index == lax.axis_size("xr") - 1).astype(jnp.float32)

    def rims(field):
        theta_ext = extended(field, (("theta", 3),), 1, True)
        axial_ext = extended(field, (("xr", 4),), 1, False)
        return (theta_ext, axial_ext)

    def advance(field, theta_ext, axial_ext, factor):
        result = local_residual(
            field, theta_ext, axial_ext, freqs, source, sigma, passage_matrix, a_axial, a_radial
        )
        return state - factor * step_size * result

    theta_ext, axial_ext = rims(state)
    first = advance(state, theta_ext, axial_ext, 0.5)
    theta_ext, axial_ext = rims(first)
    second = advance(first, theta_ext, axial_ext, 1.0)
    inlet = is_first * jnp.einsum(
        "v,hpvtr->hptr", l_rows[0], second[:, :, :, :, 0], precision=highest
    )
    outlet = is_last * jnp.einsum(
        "v,hpvtr->hptr", l_rows[1], second[:, :, :, :, caxial - 1], precision=highest
    )
    plane_values = jnp.stack([inlet, outlet], axis=1)
    cells = lax.axis_index("theta") * ctheta + jnp.arange(ctheta)
    angle = (
        2.0
        * math.pi
        * jnp.mod(mode_order[:, :, None] * cells[None, None, :], total_theta).astype(jnp.float32)
        / total_theta
    )
    cos_table = jnp.cos(angle)
    sin_table = jnp.sin(angle)
    radial_pos = jnp.arange(nradial).astype(jnp.float32) + 0.5
    radial_table = jnp.where(
        mode_radial[:, :, None] == 0,
        1.0,
        math.sqrt(2.0)
        * jnp.cos(
            math.pi
            * mode_radial[:, :, None].astype(jnp.float32)
            * radial_pos[None, None, :]
            / nradial
        ),
    )
    projected = jnp.einsum("hbptr,hkr->hbptk", plane_values, radial_table, precision=highest)
    part_real = scale * (
        jnp.einsum("hbtk,hkt->hbk", projected[:, :, 0], cos_table, precision=highest)
        + jnp.einsum("hbtk,hkt->hbk", projected[:, :, 1], sin_table, precision=highest)
    )
    part_imag = scale * (
        jnp.einsum("hbtk,hkt->hbk", projected[:, :, 1], cos_table, precision=highest)
        - jnp.einsum("hbtk,hkt->hbk", projected[:, :, 0], sin_table, precision=highest)
    )
    amp_real, amp_imag = lax.psum((part_real, part_imag), ("theta", "xr"))
    weight = (mode_plane[:, None, :] == jnp.arange(2)[None, :, None]).astype(jnp.float32)
    miss_real = weight * (amp_real - gust[:, 0][:, None, :])
    miss_imag = weight * (amp_imag - gust[:, 1][:, None, :])
    coef_real = (
        miss_real[..., None] * cos_table[:, None] - miss_imag[..., None] * sin_table[:, None]
    )
    coef_imag = (
        miss_real[..., None] * sin_table[:, None] + miss_imag[..., None] * cos_table[:, None]
    )
    corr_real = jnp.einsum("hbkt,hkr->hbtr", coef_real, radial_table, precision=highest)
    corr_imag = jnp.einsum("hbkt,hkr->hbtr", coef_imag, radial_table, precision=highest)
    correction = scale * jnp.stack([corr_real, corr_imag], axis=2)
    measured = jnp.stack([weight * amp_real, weight * amp_imag], axis=2)
    corr_in, corr_out, measured = (
        is_first * correction[:, 0],
        is_last * correction[:, 1],
        measured,
    )
    second = second.at[:, :, :, :, 0, :].add(
        -r_cols[0][None, None, :, None, None] * corr_in[:, :, None]
    )
    second = second.at[:, :, :, :, caxial - 1, :].add(
        -r_cols[1][None, None, :, None, None] * corr_out[:, :, None]
    )
    return (second, measured)


def solution(mesh):
    placed = (
        P(None, None, None, "theta", "xr", None),
        P(None, None, None, "theta", "xr", None),
        P("theta", "xr", None),
        P("theta"),
        P(),
        P(),
        P(),
        P(),
        P(),
        P(),
        P(),
        P(),
        P(),
    )
    return jax.shard_map(
        local,
        mesh=mesh,
        in_specs=placed,
        out_specs=(P(None, None, None, "theta", "xr", None), P()),
        check_vma=False,
    )
```

profile of v0, /device:TPU:0, one launch (start us, length us, event | category | flops | bytes accessed | tf_op | source)
XLA Modules:
  0.0 101.0 jit_solution(113327636697454348)
XLA Ops:
  0.6 1.8 %copy.64 = f32[3,2,5,8,8,128]{5,2,4,3,1,0:T(8,128)S(1)} copy(f32[3,2,5,8,8,128]{5,4,3,2,1,0:T(8,128)} %param.17) | data formatting | bytes 1966080 | tf_op args[0]
  3.2 5.4 %collective-permute-start = (f32[3,2,5,1,8,128]{5,2,4,3,1,0:T(8,128)}, f32[3,2,5,1,8,128]{5,2,4,3,1,0:T(8,128)S(1)}, u32[]{:S(2)}, u32[]{:S(2)}) collective-permute-start(f32[3,2,5,1,8,128]{5,2,4,3,1,0:T(8,128)} %get-tuple-element.47), channel_id=1, source_target_pairs={{2,0},{4,2},{6,4},{8,6},{10,8},{12,10},{14,12},{16,14},{18,16},{20... | collective-permute-start | bytes 368648 | tf_op jit(solution)/shard_map/ppermute | solution.py:22
  9.5 1.3 %collective-permute-start.2 = (f32[3,2,5,8,1,128]{5,2,4,3,1,0:T(8,128)}, f32[3,2,5,8,1,128]{5,2,4,3,1,0:T(8,128)}, u32[]{:S(2)}, u32[]{:S(2)}) collective-permute-start(f32[3,2,5,8,1,128]{5,2,4,3,1,0:T(8,128)} %get-tuple-element.45), channel_id=1, source_target_pairs={{1,0},{3,2},{5,4},{7,6},{9,8},{11,10},{13,12},{15,14},{17,16},{19,... | collective-permute-start | bytes 368648 | tf_op jit(solution)/shard_map/ppermute | solution.py:22
  10.8 6.0 %collective-permute-start.3 = (f32[3,2,5,8,1,128]{5,2,4,3,1,0:T(8,128)}, f32[3,2,5,8,1,128]{5,2,4,3,1,0:T(8,128)}, u32[]{:S(2)}, u32[]{:S(2)}) collective-permute-start(f32[3,2,5,8,1,128]{5,2,4,3,1,0:T(8,128)} %get-tuple-element.44), channel_id=1, source_target_pairs={{0,1},{2,3},{4,5},{6,7},{8,9},{10,11},{12,13},{14,15},{16,17},{18,... | collective-permute-start | bytes 368648 | tf_op jit(solution)/shard_map/ppermute | solution.py:21
  16.8 1.3 %slice_negate_fusion.1 = (f32[3,1,5,8,8,128]{5,2,4,3,1,0:T(8,128)}, f32[3,1,5,8,8,128]{5,2,4,3,1,0:T(8,128)}) fusion(f32[3,2,5,8,8,128]{5,2,4,3,1,0:T(8,128)S(1)} %copy.64), kind=kLoop, calls=%fused_computation.56 | loop fusion | flops 122880 | bytes 1966080 | tf_op jit(solution)/shard_map/neg | solution.py:39
  19.8 2.0 %fusion.22 = f32[3,2,8,8,128,5]{4,5,3,2,1,0:T(8,128)S(1)} fusion(f32[3,2,5,8,8,128]{5,2,4,3,1,0:T(8,128)S(1)} %copy.64, f32[5,5]{1,0:T(8,128)S(1)} %copy-done.10), kind=kOutput, calls=%fused_computation.43 | convolution fusion | flops 15237120 | bytes 1966180 | tf_op jit(solution)/shard_map/vw,hpwtxr->hpvtxr/dot_general | solution.py:45
  23.3 1.3 %negate_bitcast_fusion = (f32[5]{0:T(128)}, f32[5]{0:T(128)}) fusion(f32[2,5]{1,0:T(2,128)} %param.29), kind=kLoop, calls=%fused_computation.157 | loop fusion | flops 10 | bytes 80 | tf_op jit(solution)/shard_map/neg | solution.py:156
  24.6 1.4 %fusion.92 = (f32[3,128,8]{1,2,0:T(8,128)}, f32[3,128,8]{1,2,0:T(8,128)}) fusion(s32[8]{0:T(128)S(1)} %iota_add_fusion, s32[3,128]{1,0:T(4,128)} %param.24), kind=kLoop, calls=%fused_computation.136 | loop fusion | flops 43008 | bytes 26144 | tf_op jit(solution)/shard_map/cos | solution.py:110
  28.5 1.5 %fusion.30 = f32[3,2,5,2,4,8,128]{6,2,5,4,1,0,3:T(8,128)S(1)} fusion(f32[3,2,5,2,4,8,128]{6,2,5,4,3,1,0:T(8,128)S(1)} %bitcast.130, f32[2,5,5,1,1,1,1]{2,0,1,6,5,4,3:T(2,128)S(1)} %convolution_bitcast_fusion.2), kind=kOutput, calls=%fused_computation.50 | convolution fusion | flops 14745600 | bytes 1966280 | tf_op jit(solution)/shard_map/kvw,hpwkcxr->hpvkcxr/dot_general | solution.py:41
  30.2 0.9 copy-done.2
  31.3 5.3 %fusion.1 = f32[3,2,5,8,8,128]{5,2,4,3,1,0:T(8,128)S(1)} fusion(f32[3,2,5,8,8,128]{5,2,4,3,1,0:T(8,128)S(1)} %copy.64, f32[3,2,5,8,8,128]{5,4,3,2,1,0:T(8,128)S(1)} %copy-done.20, f32[3,1,5,8,8,128]{5,2,4,3,1,0:T(8,128)S(1)} %copy-done.3, f32[3,1,5,8,8,128]{5,2,4,3,1,0:T(8,128)S(1)} %copy-done.2, f32[3,2,8,8,128,5]{4,5,3,2,1,0:T(8,128)S(1)} %fusion.22, ...), kind=kOutput, calls=%fused_computation.7 | convolution fusion | flops 21872640 | bytes 10490368 | tf_op jit(solution)/shard_map/vw,hpwtxr->hpvtxr/dot_general | solution.py:44
  36.9 2.0 %fusion.14 = f32[3,2,8,8,128,5]{4,5,3,2,1,0:T(8,128)S(1)} fusion(f32[3,2,5,8,8,128]{5,2,4,3,1,0:T(8,128)S(1)} %fusion.1, f32[5,5]{1,0:T(8,128)S(1)} %copy-done.10), kind=kOutput, calls=%fused_computation.35 | convolution fusion | flops 15237120 | bytes 1966180 | tf_op jit(solution)/shard_map/vw,hpwtxr->hpvtxr/dot_general | solution.py:45
  38.9 4.1 %collective-permute-start.4 = (f32[3,2,5,1,8,128]{5,2,4,3,1,0:T(8,128)S(1)}, f32[3,2,5,1,8,128]{5,2,4,3,1,0:T(8,128)S(1)}, u32[]{:S(2)}, u32[]{:S(2)}) collective-permute-start(f32[3,2,5,1,8,128]{5,2,4,3,1,0:T(8,128)S(1)} %get-tuple-element.41), channel_id=1, source_target_pairs={{2,0},{4,2},{6,4},{8,6},{10,8},{12,10},{14,12},{16,14},{18,16},{20... | collective-permute-start | bytes 368648 | tf_op jit(solution)/shard_map/ppermute | solution.py:22
  43.1 1.3 %collective-permute-start.6 = (f32[3,2,5,8,1,128]{5,2,4,3,1,0:T(8,128)S(1)}, f32[3,2,5,8,1,128]{5,2,4,3,1,0:T(8,128)S(1)}, u32[]{:S(2)}, u32[]{:S(2)}) collective-permute-start(f32[3,2,5,8,1,128]{5,2,4,3,1,0:T(8,128)S(1)} %get-tuple-element.39), channel_id=1, source_target_pairs={{1,0},{3,2},{5,4},{7,6},{9,8},{11,10},{13,12},{15,14},{17,16},{19,... | collective-permute-start | bytes 368648 | tf_op jit(solution)/shard_map/ppermute | solution.py:22
  44.4 4.6 %collective-permute-start.7 = (f32[3,2,5,8,1,128]{5,2,4,3,1,0:T(8,128)S(1)}, f32[3,2,5,8,1,128]{5,2,4,3,1,0:T(8,128)S(1)}, u32[]{:S(2)}, u32[]{:S(2)}) collective-permute-start(f32[3,2,5,8,1,128]{5,2,4,3,1,0:T(8,128)S(1)} %get-tuple-element.38), channel_id=1, source_target_pairs={{0,1},{2,3},{4,5},{6,7},{8,9},{10,11},{12,13},{14,15},{16,17},{18,... | collective-permute-start | bytes 368648 | tf_op jit(solution)/shard_map/ppermute | solution.py:21
  49.0 1.9 %collective-permute-done.5 = f32[3,2,5,1,8,128]{5,2,4,3,1,0:T(8,128)S(1)} collective-permute-done((f32[3,2,5,1,8,128]{5,2,4,3,1,0:T(8,128)S(1)}, f32[3,2,5,1,8,128]{5,2,4,3,1,0:T(8,128)S(1)}, u32[]{:S(2)}, u32[]{:S(2)}) %collective-permute-start.5) | collective-permute-done | bytes 122912 | tf_op jit(solution)/shard_map/ppermute | solution.py:21
  51.1 1.5 %fusion.33 = f32[3,2,5,2,4,8,128]{6,2,5,4,1,0,3:T(8,128)S(1)} fusion(f32[3,2,5,2,4,8,128]{6,2,5,4,3,1,0:T(8,128)S(1)} %bitcast.129, f32[2,5,5,1,1,1,1]{2,0,1,6,5,4,3:T(2,128)S(1)} %convolution_bitcast_fusion.2), kind=kOutput, calls=%fused_computation.51 | convolution fusion | flops 14745600 | bytes 1966280 | tf_op jit(solution)/shard_map/kvw,hpwkcxr->hpvkcxr/dot_general | solution.py:41
  52.7 1.1 %copy-done.1 = f32[3,2,5,8,8,128]{5,4,3,2,1,0:T(8,128)S(1)} copy-done((f32[3,2,5,8,8,128]{5,4,3,2,1,0:T(8,128)S(1)}, f32[3,2,5,8,8,128]{5,4,3,2,1,0:T(8,128)}, u32[]{:S(2)}) %copy-start.1) | copy-done | bytes 983064
  53.9 4.2 %fusion.3 = f32[3,2,5,8,8,128]{5,2,4,3,1,0:T(8,128)S(1)} fusion(f32[3,2,5,8,8,128]{5,4,3,2,1,0:T(8,128)S(1)} %copy-done.20, f32[3,1,5,8,8,128]{5,2,4,3,1,0:T(8,128)S(1)} %get-tuple-element.43, f32[3,1,5,8,8,128]{5,2,4,3,1,0:T(8,128)S(1)} %get-tuple-element.42, f32[3,2,8,8,128,5]{4,5,3,2,1,0:T(8,128)S(1)} %fusion.14, ...), kind=kOutput, calls=%fused_computation.9 | convolution fusion | flops 21872640 | bytes 12063232 | tf_op jit(solution)/shard_map/vw,hpwtxr->hpvtxr/dot_general | solution.py:44
  58.7 1.1 %fusion.42 = f32[3,2,2,8,128]{4,3,2,1,0:T(8,128)S(1)} fusion(f32[128]{0:T(128)S(1)} %copy-done.22, f32[3,128]{1,0:T(4,128)S(1)} %copy-done.18, pred[3,128]{1,0:T(4,128)(4,1)S(1)} %copy-done.19, f32[3,1,2,8,128]{4,3,2,1,0:T(8,128)S(1)} %get-tuple-element.66, f32[3,1,2,8,128]{4,3,2,1,0:T(8,128)S(1)} %get-tuple-element.67), kind=kOutput, calls=%fused_computation.65 | convolution fusion | flops 19083264 | bytes 100736 | tf_op jit(solution)/shard_map/hbptr,hkr->hbptk/dot_general | solution.py:124
  60.0 37.0 %all-reduce.2 = (f32[3,2,128]{2,1,0:T(2,128)S(1)}, f32[3,2,128]{2,1,0:T(2,128)S(1)}) all-reduce(f32[3,2,128]{2,1,0:T(2,128)S(1)} %multiply_bitcast_fusion.2, f32[3,2,128]{2,1,0:T(2,128)S(1)} %multiply_bitcast_fusion.3), channel_id=1, replica_groups=mesh['theta'=16,'xr'=2] {'theta','xr'}, use_global_device_ids=true, to_apply=%region_1.2 | all-reduce | flops 1536 | bytes 12288 | tf_op jit(solution)/shard_map/psum | solution.py:133
  97.0 1.0 %convolution_bitcast_fusion.1 = f32[3,2,1,8,128]{4,3,1,0,2:T(8,128)S(1)} fusion(f32[128]{0:T(128)S(1)} %copy-done.22, f32[3,128]{1,0:T(4,128)S(1)} %copy-done.18, pred[3,128]{1,0:T(4,128)(4,1)S(1)} %copy-done.19, f32[3,128,8]{1,2,0:T(8,128)S(1)} %copy-done.5, f32[3,2,128]{2,1,0:T(2,128)S(1)} %get-tuple-element.62, f32[3,128,8]{1,2,0:T(8,128)S(1)} %copy-done.4, ...), kind=kOutput, calls=%fused_computation.53 | convolution fusion | flops 9652224 | bytes 57728 | tf_op jit(solution)/shard_map/hbkt,hkr->hbtr/dot_general | solution.py:143
  98.0 1.0 %convolution_bitcast_fusion = f32[3,2,1,8,128]{4,3,1,0,2:T(8,128)S(1)} fusion(f32[128]{0:T(128)S(1)} %copy-done.22, f32[3,128]{1,0:T(4,128)S(1)} %copy-done.18, pred[3,128]{1,0:T(4,128)(4,1)S(1)} %copy-done.19, f32[3,128,8]{1,2,0:T(8,128)S(1)} %copy-done.5, f32[3,2,128]{2,1,0:T(2,128)S(1)} %get-tuple-element.62, f32[3,128,8]{1,2,0:T(8,128)S(1)} %copy-done.4, ...), kind=kOutput, calls=%fused_computation.52 | convolution fusion | flops 9652224 | bytes 57728 | tf_op jit(solution)/shard_map/hbkt,hkr->hbtr/dot_general | solution.py:144
  99.3 1.1 %copy.68 = f32[3,2,5,8,8,128]{5,4,3,2,1,0:T(8,128)} copy(f32[3,2,5,8,8,128]{5,2,4,3,1,0:T(8,128)S(1)} %fusion.40) | data formatting | bytes 1966080
  (85 shorter events, 9.8 us)
Async XLA Ops:
  0.6 26.6 %copy-start = (f32[4,5,5]{2,0,1:T(4,128)S(1)}, f32[4,5,5]{2,0,1:T(4,128)}, u32[]{:S(2)}) copy-start(f32[4,5,5]{2,0,1:T(4,128)} %param.21) | copy-start | bytes 1204
  3.2 24.8 %collective-permute-start = (f32[3,2,5,1,8,128]{5,2,4,3,1,0:T(8,128)}, f32[3,2,5,1,8,128]{5,2,4,3,1,0:T(8,128)S(1)}, u32[]{:S(2)}, u32[]{:S(2)}) collective-permute-start(f32[3,2,5,1,8,128]{5,2,4,3,1,0:T(8,128)} %get-tuple-element.47), channel_id=1, source_target_pairs={{2,0},{4,2},{6,4},{8,6},{10,8},{12,10},{14,12},{16,14},{18,16},{20... | collective-permute-start | bytes 368648 | tf_op jit(solution)/shard_map/ppermute | solution.py:22
  8.7 19.4 %collective-permute-start.1 = (f32[3,2,5,1,8,128]{5,2,4,3,1,0:T(8,128)}, f32[3,2,5,1,8,128]{5,2,4,3,1,0:T(8,128)S(1)}, u32[]{:S(2)}, u32[]{:S(2)}) collective-permute-start(f32[3,2,5,1,8,128]{5,2,4,3,1,0:T(8,128)} %get-tuple-element.46), channel_id=1, source_target_pairs={{0,2},{2,4},{4,6},{6,8},{8,10},{10,12},{12,14},{14,16},{16,18},{18... | collective-permute-start | bytes 368648 | tf_op jit(solution)/shard_map/ppermute | solution.py:21
  9.5 20.7 %collective-permute-start.2 = (f32[3,2,5,8,1,128]{5,2,4,3,1,0:T(8,128)}, f32[3,2,5,8,1,128]{5,2,4,3,1,0:T(8,128)}, u32[]{:S(2)}, u32[]{:S(2)}) collective-permute-start(f32[3,2,5,8,1,128]{5,2,4,3,1,0:T(8,128)} %get-tuple-element.45), channel_id=1, source_target_pairs={{1,0},{3,2},{5,4},{7,6},{9,8},{11,10},{13,12},{15,14},{17,16},{19,... | collective-permute-start | bytes 368648 | tf_op jit(solution)/shard_map/ppermute | solution.py:22
  10.8 7.9 %copy-start.13 = (s32[3,128]{1,0:T(4,128)S(1)}, s32[3,128]{1,0:T(4,128)}, u32[]{:S(2)}) copy-start(s32[3,128]{1,0:T(4,128)} %param.25) | copy-start | bytes 4612
  10.8 9.1 %copy-start.10 = (f32[5,5]{1,0:T(8,128)S(1)}, f32[5,5]{1,0:T(8,128)}, u32[]{:S(2)}) copy-start(f32[5,5]{1,0:T(8,128)} %param.23) | copy-start | bytes 304
  10.8 19.4 %collective-permute-start.3 = (f32[3,2,5,8,1,128]{5,2,4,3,1,0:T(8,128)}, f32[3,2,5,8,1,128]{5,2,4,3,1,0:T(8,128)}, u32[]{:S(2)}, u32[]{:S(2)}) collective-permute-start(f32[3,2,5,8,1,128]{5,2,4,3,1,0:T(8,128)} %get-tuple-element.44), channel_id=1, source_target_pairs={{0,1},{2,3},{4,5},{6,7},{8,9},{10,11},{12,13},{14,15},{16,17},{18,... | collective-permute-start | bytes 368648 | tf_op jit(solution)/shard_map/ppermute | solution.py:21
  19.8 2.0 %copy-start.6 = (f32[8,8,128]{2,1,0:T(8,128)S(1)}, f32[8,8,128]{2,1,0:T(8,128)}, u32[]{:S(2)}) copy-start(f32[8,8,128]{2,1,0:T(8,128)} %param.19) | copy-start | bytes 98308
  28.5 1.7 %copy-start.20 = (f32[3,2,5,8,8,128]{5,4,3,2,1,0:T(8,128)S(1)}, f32[3,2,5,8,8,128]{5,4,3,2,1,0:T(8,128)}, u32[]{:S(2)}) copy-start(f32[3,2,5,8,8,128]{5,4,3,2,1,0:T(8,128)} %param.18) | copy-start | bytes 2949124
  38.9 10.0 %collective-permute-start.4 = (f32[3,2,5,1,8,128]{5,2,4,3,1,0:T(8,128)S(1)}, f32[3,2,5,1,8,128]{5,2,4,3,1,0:T(8,128)S(1)}, u32[]{:S(2)}, u32[]{:S(2)}) collective-permute-start(f32[3,2,5,1,8,128]{5,2,4,3,1,0:T(8,128)S(1)} %get-tuple-element.41), channel_id=1, source_target_pairs={{2,0},{4,2},{6,4},{8,6},{10,8},{12,10},{14,12},{16,14},{18,16},{20... | collective-permute-start | bytes 368648 | tf_op jit(solution)/shard_map/ppermute | solution.py:22
  43.1 7.8 %collective-permute-start.5 = (f32[3,2,5,1,8,128]{5,2,4,3,1,0:T(8,128)S(1)}, f32[3,2,5,1,8,128]{5,2,4,3,1,0:T(8,128)S(1)}, u32[]{:S(2)}, u32[]{:S(2)}) collective-permute-start(f32[3,2,5,1,8,128]{5,2,4,3,1,0:T(8,128)S(1)} %get-tuple-element.40), channel_id=1, source_target_pairs={{0,2},{2,4},{4,6},{6,8},{8,10},{10,12},{12,14},{14,16},{16,18},{18... | collective-permute-start | bytes 368648 | tf_op jit(solution)/shard_map/ppermute | solution.py:21
  43.1 9.6 %collective-permute-start.6 = (f32[3,2,5,8,1,128]{5,2,4,3,1,0:T(8,128)S(1)}, f32[3,2,5,8,1,128]{5,2,4,3,1,0:T(8,128)S(1)}, u32[]{:S(2)}, u32[]{:S(2)}) collective-permute-start(f32[3,2,5,8,1,128]{5,2,4,3,1,0:T(8,128)S(1)} %get-tuple-element.39), channel_id=1, source_target_pairs={{1,0},{3,2},{5,4},{7,6},{9,8},{11,10},{13,12},{15,14},{17,16},{19,... | collective-permute-start | bytes 368648 | tf_op jit(solution)/shard_map/ppermute | solution.py:22
  44.4 8.3 %collective-permute-start.7 = (f32[3,2,5,8,1,128]{5,2,4,3,1,0:T(8,128)S(1)}, f32[3,2,5,8,1,128]{5,2,4,3,1,0:T(8,128)S(1)}, u32[]{:S(2)}, u32[]{:S(2)}) collective-permute-start(f32[3,2,5,8,1,128]{5,2,4,3,1,0:T(8,128)S(1)} %get-tuple-element.38), channel_id=1, source_target_pairs={{0,1},{2,3},{4,5},{6,7},{8,9},{10,11},{12,13},{14,15},{16,17},{18,... | collective-permute-start | bytes 368648 | tf_op jit(solution)/shard_map/ppermute | solution.py:21
  53.8 4.3 %copy-start.14 = (f32[2,5]{1,0:T(2,128)S(1)}, f32[2,5]{1,0:T(2,128)}, u32[]{:S(2)}) copy-start(f32[2,5]{1,0:T(2,128)} %param.28) | copy-start | bytes 124
  53.8 4.9 %copy-start.18 = (f32[3,128]{1,0:T(4,128)S(1)}, f32[3,128]{1,0:T(4,128)}, u32[]{:S(2)}) copy-start(f32[3,128]{1,0:T(4,128)} %convert_multiply_fusion) | copy-start | bytes 4612
  53.8 4.9 %copy-start.19 = (pred[3,128]{1,0:T(4,128)(4,1)S(1)}, pred[3,128]{1,0:T(4,128)(4,1)}, u32[]{:S(2)}) copy-start(pred[3,128]{1,0:T(4,128)(4,1)} %broadcast_compare_fusion) | copy-start | bytes 1156
  53.8 4.9 %copy-start.22 = (f32[128]{0:T(128)S(1)}, f32[128]{0:T(128)}, u32[]{:S(2)}) copy-start(f32[128]{0:T(128)} %convert_add_fusion) | copy-start | bytes 1540
  53.8 6.1 %copy-start.4 = (f32[3,128,8]{1,2,0:T(8,128)S(1)}, f32[3,128,8]{1,2,0:T(8,128)}, u32[]{:S(2)}) copy-start(f32[3,128,8]{1,2,0:T(8,128)} %get-tuple-element.60) | copy-start | bytes 36868
  53.8 6.1 %copy-start.5 = (f32[3,128,8]{1,2,0:T(8,128)S(1)}, f32[3,128,8]{1,2,0:T(8,128)}, u32[]{:S(2)}) copy-start(f32[3,128,8]{1,2,0:T(8,128)} %get-tuple-element.61) | copy-start | bytes 36868
  53.8 43.1 %copy-start.11 = (f32[3,128]{1,0:T(4,128)S(1)}, f32[3,128]{1,0:T(4,128)}, u32[]{:S(2)}) copy-start(f32[3,128]{1,0:T(4,128)} %get-tuple-element.68) | copy-start | bytes 4612
  53.8 43.1 %copy-start.12 = (f32[3,128]{1,0:T(4,128)S(1)}, f32[3,128]{1,0:T(4,128)}, u32[]{:S(2)}) copy-start(f32[3,128]{1,0:T(4,128)} %get-tuple-element.69) | copy-start | bytes 4612
  53.8 43.1 %copy-start.17 = (s32[3,128]{1,0:T(4,128)S(1)}, s32[3,128]{1,0:T(4,128)}, u32[]{:S(2)}) copy-start(s32[3,128]{1,0:T(4,128)} %param.26) | copy-start | bytes 4612
  58.1 41.0 %copy-start.16 = (f32[5]{0:T(128)S(1)}, f32[5]{0:T(128)}, u32[]{:S(2)}) copy-start(f32[5]{0:T(128)} %get-tuple-element.65) | copy-start | bytes 64
  58.1 41.1 %copy-start.15 = (f32[5]{0:T(128)S(1)}, f32[5]{0:T(128)}, u32[]{:S(2)}) copy-start(f32[5]{0:T(128)} %get-tuple-element.64) | copy-start | bytes 64
  (8 other events, 10.3 us)
where the time goes:
time: 102 us; the launch traced here: 101 us
  blocking collectives  37 us (36%)
  starting transfers between devices  22.7 us (22%)
  matrix products  21.1 us (21%)
  other arithmetic  8.76 us (9%)
  local copies, waits for them, and re-layouts  8.44 us (8%)
  waiting for transfers between devices  1.88 us (2%)
  between operations  1.16 us (1%)
    psum x1, blocking collectives, local(): amp_real, amp_imag = lax.psum((part_real, part_imag), ('theta', 'xr'))  37 us
    ppermute x4, starting transfers between devices, extended(): after = lax.ppermute(initial, axis, down)  12.1 us
    ppermute x4, starting transfers between devices, extended(): before = lax.ppermute(last, axis, up)  10.6 us
    dot_general x2, matrix products, local_residual(): jnp.einsum('vw,hpwtxr->hpvtxr', a_axial, diff_axial, precision=highest)  9.49 us
    unnamed x51, local copies, waits for them, and re-layouts  5.77 us
    dot_general x2, matrix products, local_residual(): jnp.einsum('vw,hpwtxr->hpvtxr', a_radial, diff_radial, precision=highest)  4.07 us
    dot_general x2, matrix products, local_residual(): jnp.einsum('kvw,hpwkcxr->hpvkcxr', passage_matrix, grouped, precision=hig...  2.91 us
  transfers between devices with their start and end apart: 8, of which 1 were waited for; matrix products, arithmetic and copies ran while one was open for 16% of the time, Pallas kernels for 0%

commit v1 on v0

v1 whole, which is shorter than its diff:
```python
import functools
import math

import jax
import jax.numpy as jnp
from jax import lax
from jax.experimental import pallas as pl
from jax.experimental.pallas import tpu as pltpu
from jax.sharding import PartitionSpec as P

courant = 0.5
viscosity = 0.1
base_frequency = 0.5
highest = lax.Precision.HIGHEST
MESH = pl.DeviceIdType.MESH


def kernel(
    dims,
    state_hbm,
    source_hbm,
    sigma_hbm,
    stagger,
    a_theta,
    a_axial,
    a_radial,
    mode_order,
    mode_radial,
    mode_plane,
    gust,
    l_rows,
    r_cols,
    out,
    amps,
    state,
    source,
    sigma,
    first,
    step,
    thalo,
    xhalo,
    xsend,
    phi,
    cosines,
    sines,
    part,
    parts,
    load_sem,
    tsend_sem,
    trecv_sem,
    xsend_sem,
    xrecv_sem,
    psend_sem,
    precv_sem,
):
    T, X, H, V, CT, CX, NR, NPASS, NMODE = dims
    F = 2 * V
    CPP = CT // NPASS
    N = T * X
    th = lax.axis_index("theta")
    xr = lax.axis_index("xr")
    me = th * X + xr
    up = lax.rem(th + 1, T)
    down = lax.rem(th + T - 1, T)
    has_lo = xr > 0
    has_hi = xr < X - 1
    total_theta = CT * T
    scale = 1.0 / math.sqrt(total_theta * NR)

    barrier = pltpu.get_barrier_semaphore()

    @pl.loop(1, N)
    def _(i):
        other = lax.rem(me + i, N)
        pl.semaphore_signal(
            barrier, inc=1, device_id=(other // X, lax.rem(other, X)), device_id_type=MESH
        )

    loads = [
        pltpu.make_async_copy(state_hbm, state.at[:, pl.ds(CX, CT * CX)], load_sem.at[0]),
        pltpu.make_async_copy(sigma_hbm, sigma, load_sem.at[1]),
        pltpu.make_async_copy(source_hbm, source, load_sem.at[2]),
    ]
    for copy in loads:
        copy.start()

    zero = jnp.zeros((H * F, CX, NR), jnp.float32)
    for buf in (state, first):
        buf[:, pl.ds(0, CX)] = zero
        buf[:, pl.ds(CX + CT * CX, CX)] = zero

    def x_rows(row):
        return pl.ds(row, CT, stride=CX)

    loads[0].wait()
    for h in range(H):
        for f in range(F):
            xsend[0, 0, h, f] = state[h * F + f, x_rows(CX + CX - 1), :]
            xsend[0, 1, h, f] = state[h * F + f, x_rows(CX), :]

    pl.semaphore_wait(barrier, N - 1)

    def t_copies(src, offset, stage, h):
        rows = pl.ds(h * F, F)
        return [
            pltpu.make_async_remote_copy(
                src_ref=src.at[rows, pl.ds(offset + (CT - 1) * CX, CX)],
                dst_ref=thalo.at[stage, 0, h],
                send_sem=tsend_sem.at[stage, 0, h],
                recv_sem=trecv_sem.at[stage, 0, h],
                device_id=(up, xr),
                device_id_type=MESH,
            ),
            pltpu.make_async_remote_copy(
                src_ref=src.at[rows, pl.ds(offset, CX)],
                dst_ref=thalo.at[stage, 1, h],
                send_sem=tsend_sem.at[stage, 1, h],
                recv_sem=trecv_sem.at[stage, 1, h],
                device_id=(down, xr),
                device_id_type=MESH,
            ),
        ]

    def x_copy(stage, side, h):
        target = xr + 1 if side == 0 else xr - 1
        return pltpu.make_async_remote_copy(
            src_ref=xsend.at[stage, side, h],
            dst_ref=xhalo.at[stage, side, h],
            send_sem=xsend_sem.at[stage, side, h],
            recv_sem=xrecv_sem.at[stage, side, h],
            device_id=(th, target),
            device_id_type=MESH,
        )

    def send(stage, h):
        for copy in t_copies(state_hbm if stage == 0 else first, 0 if stage == 0 else CX, stage, h):
            copy.start()

        @pl.when(has_hi)
        def _():
            x_copy(stage, 0, h).start()

        @pl.when(has_lo)
        def _():
            x_copy(stage, 1, h).start()

    for h in range(H):
        send(0, h)

    loads[1].wait()
    step[...] = courant / (1.0 + sigma[...])
    loads[2].wait()

    row_id = lax.broadcasted_iota(jnp.int32, (CX, NR), 0)
    lane_id = lax.broadcasted_iota(jnp.int32, (CX, NR), 1)
    first_row = row_id == 0
    last_row = row_id == CX - 1
    first_lane = lane_id == 0
    last_lane = lane_id == NR - 1

    def main(field, result, result_offset, factor):
        @pl.loop(0, H)
        def _(h):
            freq = base_frequency * (h + 1).astype(jnp.float32)

            @pl.loop(0, CT)
            def _(t):
                base = pl.multiple_of(t * CX, CX)
                kind = stagger[t // CPP]
                dt = step[pl.ds(base, CX)]
                if factor != 1.0:
                    dt = factor * dt
                damp = sigma[pl.ds(base, CX)] + 6.0 * viscosity
                at = [[a_theta[kind, v, w] for w in range(V)] for v in range(V)]
                for p in range(2):
                    flux = [None] * V
                    sums = []
                    for w in range(V):
                        f = h * F + p * V + w
                        u = field[f, pl.ds(base + CX, CX)]
                        tm = field[f, pl.ds(base, CX)]
                        tp = field[f, pl.ds(base + 2 * CX, CX)]
                        xm = jnp.where(first_row, 0.0, pltpu.roll(u, 1, 0))
                        xp = jnp.where(last_row, 0.0, pltpu.roll(u, CX - 1, 0))
                        rm = jnp.where(first_lane, 0.0, pltpu.roll(u, 1, 1))
                        rp = jnp.where(last_lane, 0.0, pltpu.roll(u, NR - 1, 1))
                        dth, dx, dr = tp - tm, xp - xm, rp - rm
                        sums.append(((tp + tm) + (xp + xm)) + (rp + rm))
                        for v in range(V):
                            term = (
                                at[v][w] * dth + a_axial[v, w] * dx + a_radial[v, w] * dr
                            )
                            flux[v] = term if flux[v] is None else flux[v] + term
                    for v in range(V):
                        f = h * F + p * V + v
                        u = field[f, pl.ds(base + CX, CX)]
                        other = field[h * F + (1 - p) * V + v, pl.ds(base + CX, CX)]
                        turned = -freq if p == 0 else freq
                        res = (
                            0.5 * flux[v]
                            - viscosity * sums[v]
                            + damp * u
                            + turned * other
                            - source[f, pl.ds(base, CX)]
                        )
                        start = state[f, pl.ds(base + CX, CX)]
                        result[f, pl.ds(base + result_offset, CX)] = start - dt * res

    def halo_terms(values, matrix, sign):
        terms = []
        for v in range(V):
            total = matrix(v, 0) * values[0]
            for w in range(1, V):
                total = total + matrix(v, w) * values[w]
            terms.append((sign * 0.5) * total - viscosity * values[v])
        return terms

    def add_halos(result, offset, stage, h, factor):
        for side, copy in enumerate(t_copies(state_hbm, 0, stage, h)):
            copy.wait_recv()
            t = 0 if side == 0 else CT - 1
            kind = stagger[t // CPP]
            dt = factor * step[pl.ds(t * CX, CX)]
            for p in range(2):
                values = [thalo[stage, side, h, p * V + w] for w in range(V)]
                terms = halo_terms(
                    values, lambda v, w: a_theta[kind, v, w], -1.0 if side == 0 else 1.0
                )
                for v in range(V):
                    at = (h * F + p * V + v, pl.ds(offset + t * CX, CX))
                    result[at] = result[at] - dt * terms[v]
        for side in range(2):

            @pl.when(has_lo if side == 0 else has_hi)
            def _():
                x_copy(stage, side, h).wait_recv()
                x = 0 if side == 0 else CX - 1
                dt = factor * step[x_rows(x), :]
                for p in range(2):
                    values = [xhalo[stage, side, h, p * V + w] for w in range(V)]
                    terms = halo_terms(
                        values, lambda v, w: a_axial[v, w], -1.0 if side == 0 else 1.0
                    )
                    for v in range(V):
                        f = h * F + p * V + v
                        at = (f, x_rows(offset + x), slice(None))
                        result[at] = result[at] - dt * terms[v]

    main(state, first, CX, 0.5)

    cells = (th * CT + lax.broadcasted_iota(jnp.int32, (CT, NMODE), 0)).astype(jnp.float32)
    radial_pos = lax.broadcasted_iota(jnp.int32, (NR, NMODE), 0).astype(jnp.float32) + 0.5
    for h in range(H):
        turns = mode_order[pl.ds(h, 1)].astype(jnp.float32) * cells
        turns = turns - jnp.floor(turns / total_theta) * total_theta
        angle = (2.0 * math.pi) * turns / total_theta
        cosines[h] = jnp.cos(angle)
        sines[h] = jnp.sin(angle)
        radial = mode_radial[pl.ds(h, 1)]
        phi[h] = jnp.where(
            radial == 0,
            1.0,
            math.sqrt(2.0) * jnp.cos(math.pi * radial.astype(jnp.float32) * radial_pos / NR),
        )

    for h in range(H):
        add_halos(first, CX, 0, h, 0.5)
        for f in range(F):
            xsend[1, 0, h, f] = first[h * F + f, x_rows(CX + CX - 1), :]
            xsend[1, 1, h, f] = first[h * F + f, x_rows(CX), :]
        send(1, h)

    main(first, out, 0, 1.0)

    def project(b, h):
        x = 0 if b == 0 else CX - 1
        planes = []
        for p in range(2):
            total = None
            for v in range(V):
                term = l_rows[b, v] * out[h * F + p * V + v, x_rows(x), :]
                total = term if total is None else total + term
            planes.append(total)
        projected = jnp.dot(
            jnp.concatenate(planes, axis=0),
            phi[h],
            precision=highest,
            preferred_element_type=jnp.float32,
        )
        real, imag = projected[:CT], projected[CT:]
        weight = jnp.where(mode_plane[pl.ds(h, 1)] == b, scale, 0.0)
        part_real = jnp.sum(real * cosines[h] + imag * sines[h], axis=0, keepdims=True)
        part_imag = jnp.sum(imag * cosines[h] - real * sines[h], axis=0, keepdims=True)
        part[pl.ds(2 * h, 1)] = weight * part_real
        part[pl.ds(2 * h + 1, 1)] = weight * part_imag

    part[...] = jnp.zeros_like(part)
    for h in range(H):
        add_halos(out, 0, 1, h, 1.0)

        @pl.when(jnp.logical_not(has_lo))
        def _():
            project(0, h)

        @pl.when(jnp.logical_not(has_hi))
        def _():
            project(1, h)

    def part_copy(other):
        return pltpu.make_async_remote_copy(
            src_ref=part,
            dst_ref=parts.at[me],
            send_sem=psend_sem,
            recv_sem=precv_sem,
            device_id=(other // X, lax.rem(other, X)),
            device_id_type=MESH,
        )

    @pl.loop(1, N)
    def _(i):
        part_copy(lax.rem(me + i, N)).start()

    parts[me] = part[...]
    everyone = pltpu.make_async_remote_copy(
        src_ref=parts.at[pl.ds(0, N - 1)],
        dst_ref=parts.at[pl.ds(0, N - 1)],
        send_sem=psend_sem,
        recv_sem=precv_sem,
        device_id=(up, xr),
        device_id_type=MESH,
    )
    everyone.wait_recv()
    total = parts[0]
    if N <= 64:
        for i in range(1, N):
            total = total + parts[i]
    else:
        total = lax.fori_loop(1, N, lambda i, acc: acc + parts[i], total)
    part_rows = [total[i : i + 1] for i in range(2 * H)]
    for h in range(H):
        for b in range(2):
            mine = mode_plane[pl.ds(h, 1)] == b
            for p in range(2):
                amps[h, b, pl.ds(p, 1)] = jnp.where(mine, part_rows[2 * h + p], 0.0)

    def correct(b, h):
        x = 0 if b == 0 else CX - 1
        weight = jnp.where(mode_plane[pl.ds(h, 1)] == b, scale, 0.0)
        real = weight * (part_rows[2 * h] - gust[h, pl.ds(0, 1)])
        imag = weight * (part_rows[2 * h + 1] - gust[h, pl.ds(1, 1)])
        coef = jnp.concatenate(
            [real * cosines[h] - imag * sines[h], real * sines[h] + imag * cosines[h]], axis=0
        )
        q = lax.dot_general(
            coef,
            phi[h],
            (((1,), (1,)), ((), ())),
            precision=highest,
            preferred_element_type=jnp.float32,
        )
        for p in range(2):
            for v in range(V):
                at = (h * F + p * V + v, x_rows(x), slice(None))
                out[at] = out[at] - r_cols[b, v] * q[p * CT : (p + 1) * CT]

    @pl.when(jnp.logical_not(has_lo))
    def _():
        for h in range(H):
            correct(0, h)

    @pl.when(jnp.logical_not(has_hi))
    def _():
        for h in range(H):
            correct(1, h)

    everyone.wait_send()
    for stage in range(2):
        for h in range(H):
            src = state_hbm if stage == 0 else first
            for copy in t_copies(src, 0 if stage == 0 else CX, stage, h):
                copy.wait_send()

            @pl.when(has_hi)
            def _():
                x_copy(stage, 0, h).wait_send()

            @pl.when(has_lo)
            def _():
                x_copy(stage, 1, h).wait_send()


def local(T, X, *args):
    state, source, sigma, stagger = args[:4]
    H, two, V, CT, CX, NR = state.shape
    F = two * V
    NMODE = args[7].shape[1]
    dims = (T, X, H, V, CT, CX, NR, stagger.shape[0], NMODE)
    N = T * X
    rows = CT * CX
    f32 = jnp.float32
    hbm = pl.BlockSpec(memory_space=pl.ANY)
    vmem = pl.BlockSpec(memory_space=pltpu.VMEM)
    smem = pl.BlockSpec(memory_space=pltpu.SMEM)
    DMA = pltpu.SemaphoreType.DMA
    pad = -(-2 * H // 8) * 8
    fields, amplitudes = pl.pallas_call(
        functools.partial(kernel, dims),
        out_shape=(
            jax.ShapeDtypeStruct((H * F, rows, NR), f32),
            jax.ShapeDtypeStruct((H, 2, 2, NMODE), f32),
        ),
        in_specs=[hbm, hbm, hbm, smem, smem, smem, smem, vmem, vmem, vmem, vmem, smem, smem],
        out_specs=(vmem, vmem),
        scratch_shapes=[
            pltpu.VMEM((H * F, rows + 2 * CX, NR), f32),
            pltpu.VMEM((H * F, rows, NR), f32),
            pltpu.VMEM((rows, NR), f32),
            pltpu.VMEM((H * F, rows + 2 * CX, NR), f32),
            pltpu.VMEM((rows, NR), f32),
            pltpu.VMEM((2, 2, H, F, CX, NR), f32),
            pltpu.VMEM((2, 2, H, F, CT, NR), f32),
            pltpu.VMEM((2, 2, H, F, CT, NR), f32),
            pltpu.VMEM((H, NR, NMODE), f32),
            pltpu.VMEM((H, CT, NMODE), f32),
            pltpu.VMEM((H, CT, NMODE), f32),
            pltpu.VMEM((pad, NMODE), f32),
            pltpu.VMEM((N, pad, NMODE), f32),
            DMA((3,)),
            DMA((2, 2, H)),
            DMA((2, 2, H)),
            DMA((2, 2, H)),
            DMA((2, 2, H)),
            DMA,
            DMA,
        ],
        compiler_params=pltpu.CompilerParams(
            collective_id=0, has_side_effects=True, vmem_limit_bytes=40 * 2**20
        ),
        name="wake",
    )(
        state.reshape(H * F, rows, NR),
        source.reshape(H * F, rows, NR),
        sigma.reshape(rows, NR),
        *args[3:],
    )
    return fields.reshape(state.shape), amplitudes


def solution(mesh):
    field = P(None, None, None, "theta", "xr", None)
    placed = (field, field, P("theta", "xr", None), P("theta")) + (P(),) * 9
    return jax.shard_map(
        functools.partial(local, mesh.shape["theta"], mesh.shape["xr"]),
        mesh=mesh,
        in_specs=placed,
        out_specs=(field, P()),
        check_vma=False,
    )
```

time: 102 us -> 28.5 us (0.28)
  blocking collectives: 37 us -> 0 us
  starting transfers between devices: 22.7 us -> 0 us
  Pallas kernels: 0 us -> 21.9 us
  matrix products: 21.1 us -> 0 us
  other arithmetic: 8.76 us -> 0 us
  local copies, waits for them, and re-layouts: 8.44 us -> 5.49 us
  waiting for transfers between devices: 1.88 us -> 0 us
    psum x1 -> x0, blocking collectives: 37 us -> none  [local(): amp_real, amp_imag = lax.psum((part_real, part_imag), ('theta', 'xr'))]
    ppermute x8 -> x0, starting transfers between devices: 22.7 us -> none  [the longest x4 12.1 us: extended(): after = lax.ppermute(initial, axis, down)]
    pallas_call x0 -> x1, Pallas kernels: none -> 21.9 us  [local(): pl.pallas_call(functools.partial(kernel, dims), out_shape=(jax.ShapeDtype...]
    dot_general x12 -> x0, matrix products: 21.1 us -> none  [the longest x2 9.49 us: local_residual(): jnp.einsum('vw,hpwtxr->hpvtxr', a_axial, diff_axial, precision=highest)]
    neg x3 -> x0, other arithmetic: 2.81 us -> none  [the longest x2 1.48 us: local_residual(): turned = jnp.stack([-field[:, 1], field[:, 0]], axis=1)]
    slice x5 -> x0, local copies, waits for them, and re-layouts: 2.39 us -> none  [the longest x4 1.63 us: extended(): last = lax.slice_in_dim(array, length - width, length, axis=dim)]
    ppermute x8 -> x0, waiting for transfers between devices: 1.88 us -> none  [the longest x4 1.87 us: extended(): before = lax.ppermute(last, axis, up)]
    mul x9 -> x0, other arithmetic: 1.85 us -> none  [the longest x2 0.63 us: local_residual(): diff_theta = (theta_ext[:, :, :, 2:] - theta_ext[:, :, :, :-2]) * 0.5]
  transfers between devices with their start and end apart: 8 -> 0, of which waited for: 1 -> 0; matrix products, arithmetic and copies ran while one was open for 16% -> 0% of each run, Pallas kernels for 0% -> 0%
where the time goes in v1:
time: 28.5 us; the launch traced here: 28.1 us
  Pallas kernels  21.9 us (77%)
  local copies, waits for them, and re-layouts  5.49 us (19%)
  between operations  0.78 us (3%)
    pallas_call x1, Pallas kernels, local(): pl.pallas_call(functools.partial(kernel, dims), out_shape=(jax.ShapeDtype...  21.9 us
    unnamed x27, local copies, waits for them, and re-layouts  5.49 us

profile of v1, /device:TPU:0, one launch (start us, length us, event | category | flops | bytes accessed | tf_op | source)
XLA Modules:
  0.0 28.1 jit_solution(12801721541843681332)
XLA Ops:
  0.6 0.0 copy-start.3
  0.6 0.0 copy-start.4
  0.7 0.0 copy-start.5
  0.7 0.0 copy-start.6
  0.7 0.0 copy-start.7
  0.7 0.0 copy-start.8
  0.7 0.0 copy-start.9
  0.7 0.0 copy-start.10
  0.7 0.0 copy-start.11
  0.7 0.8 %copy.15.a_theta = f32[4,5,5]{2,1,0:T(8,128)S(1)} copy(f32[4,5,5]{2,0,1:T(4,128)} %param.17) | data formatting | bytes 800 | tf_op args[4]
  1.5 0.0 copy-done.3
  1.5 0.0 copy-done.6
  1.5 0.0 copy-done.7
  1.5 0.0 copy-done.8
  1.5 0.0 copy-done.9
  1.5 0.0 copy-done.10
  1.5 0.0 copy-done.11
  1.6 0.0 copy-start
  1.6 1.2 %copy-done = f32[3,2,5,8,8,128]{5,4,3,2,1,0:T(8,128)S(1)} copy-done((f32[3,2,5,8,8,128]{5,4,3,2,1,0:T(8,128)S(1)}, f32[3,2,5,8,8,128]{5,4,3,2,1,0:T(8,128)}, u32[]{:S(2)}) %copy-start) | copy-done | bytes 983064
  2.8 1.2 %copy-done.1 = f32[3,2,5,8,8,128]{5,4,3,2,1,0:T(8,128)S(1)} copy-done((f32[3,2,5,8,8,128]{5,4,3,2,1,0:T(8,128)S(1)}, f32[3,2,5,8,8,128]{5,4,3,2,1,0:T(8,128)}, u32[]{:S(2)}) %copy-start.1) | copy-done | bytes 983064
  4.0 0.8 %copy-done.2 = f32[8,8,128]{2,1,0:T(8,128)S(1)} copy-done((f32[8,8,128]{2,1,0:T(8,128)S(1)}, f32[8,8,128]{2,1,0:T(8,128)}, u32[]{:S(2)}) %copy-start.2) | copy-done | bytes 32792
  4.7 21.9 %wake.1 = (f32[30,64,128]{2,1,0:T(8,128)S(1)}, f32[3,2,2,128]{3,2,1,0:T(2,128)S(1)}) custom-call(f32[30,64,128]{2,1,0:T(8,128)S(1)} %bitcast.4, f32[30,64,128]{2,1,0:T(8,128)S(1)} %bitcast.5, f32[64,128]{1,0:T(8,128)S(1)} %bitcast.7, s32[2]{0:T(128)S(1)} %copy-done.11, f32[4,5,5]{2,1,0:T(8,128)S(1)} %copy.15.a_theta, f32[5,5]{1,0:T(8,128)S(1)} %copy-done.3, ...), custom_call_target="tpu_custom_call" | custom-call | tf_op jit(solution)/shard_map/wake/pallas_call | solution.py:406
  26.6 0.9 %copy.18 = f32[3,2,5,8,8,128]{5,4,3,2,1,0:T(8,128)} copy(f32[3,2,5,8,8,128]{5,4,3,2,1,0:T(8,128)S(1)} %bitcast.6) | data formatting | bytes 1966080
  27.5 0.6 %copy.19 = f32[3,2,2,128]{3,2,1,0:T(2,128)} copy(f32[3,2,2,128]{3,2,1,0:T(2,128)S(1)} %get-tuple-element.9) | data formatting | bytes 12288
  (4 shorter events, 0.0 us)
Async XLA Ops:
  0.6 0.8 %copy-start.3 = (f32[5,5]{1,0:T(8,128)S(1)}, f32[5,5]{1,0:T(8,128)}, u32[]{:S(2)}) copy-start(f32[5,5]{1,0:T(8,128)} %a_axial.1) | copy-start | bytes 304
  0.6 0.8 %copy-start.4 = (f32[5,5]{1,0:T(8,128)S(1)}, f32[5,5]{1,0:T(8,128)}, u32[]{:S(2)}) copy-start(f32[5,5]{1,0:T(8,128)} %a_radial.1) | copy-start | bytes 304
  0.7 0.8 %copy-start.5 = (f32[3,2,128]{2,1,0:T(2,128)S(1)}, f32[3,2,128]{2,1,0:T(2,128)}, u32[]{:S(2)}) copy-start(f32[3,2,128]{2,1,0:T(2,128)} %gust.1) | copy-start | bytes 9220
  0.7 0.8 %copy-start.6 = (s32[3,128]{1,0:T(4,128)S(1)}, s32[3,128]{1,0:T(4,128)}, u32[]{:S(2)}) copy-start(s32[3,128]{1,0:T(4,128)} %mode_order.1) | copy-start | bytes 4612
  0.7 0.8 %copy-start.7 = (s32[3,128]{1,0:T(4,128)S(1)}, s32[3,128]{1,0:T(4,128)}, u32[]{:S(2)}) copy-start(s32[3,128]{1,0:T(4,128)} %mode_radial.1) | copy-start | bytes 4612
  0.7 0.8 %copy-start.8 = (s32[3,128]{1,0:T(4,128)S(1)}, s32[3,128]{1,0:T(4,128)}, u32[]{:S(2)}) copy-start(s32[3,128]{1,0:T(4,128)} %mode_plane.1) | copy-start | bytes 4612
  0.7 0.8 %copy-start.9 = (f32[2,5]{1,0:T(2,128)S(1)}, f32[2,5]{1,0:T(2,128)}, u32[]{:S(2)}) copy-start(f32[2,5]{1,0:T(2,128)} %l_rows.1) | copy-start | bytes 124
  0.7 0.8 %copy-start.10 = (f32[2,5]{1,0:T(2,128)S(1)}, f32[2,5]{1,0:T(2,128)}, u32[]{:S(2)}) copy-start(f32[2,5]{1,0:T(2,128)} %r_cols.1) | copy-start | bytes 124
  0.7 0.8 %copy-start.11 = (s32[2]{0:T(128)S(1)}, s32[2]{0:T(128)}, u32[]{:S(2)}) copy-start(s32[2]{0:T(128)} %stagger.1) | copy-start | bytes 28
  1.6 1.2 %copy-start = (f32[3,2,5,8,8,128]{5,4,3,2,1,0:T(8,128)S(1)}, f32[3,2,5,8,8,128]{5,4,3,2,1,0:T(8,128)}, u32[]{:S(2)}) copy-start(f32[3,2,5,8,8,128]{5,4,3,2,1,0:T(8,128)} %param.13) | copy-start | bytes 2949124
  2.8 1.2 %copy-start.1 = (f32[3,2,5,8,8,128]{5,4,3,2,1,0:T(8,128)S(1)}, f32[3,2,5,8,8,128]{5,4,3,2,1,0:T(8,128)}, u32[]{:S(2)}) copy-start(f32[3,2,5,8,8,128]{5,4,3,2,1,0:T(8,128)} %param.14) | copy-start | bytes 2949124
  4.0 0.8 %copy-start.2 = (f32[8,8,128]{2,1,0:T(8,128)S(1)}, f32[8,8,128]{2,1,0:T(8,128)}, u32[]{:S(2)}) copy-start(f32[8,8,128]{2,1,0:T(8,128)} %param.15) | copy-start | bytes 98308

commit v2 on v1

--- a/solution.py
+++ b/solution.py
@@ -20,18 +20,14 @@
     state_hbm,
     source_hbm,
     sigma_hbm,
-    stagger,
-    a_theta,
-    a_axial,
-    a_radial,
-    mode_order,
-    mode_radial,
-    mode_plane,
-    gust,
-    l_rows,
-    r_cols,
-    out,
-    amps,
+    *refs,
+):
+    small_hbm, refs = refs[:10], refs[10:]
+    out, amps, refs = refs[0], refs[1], refs[2:]
+    small, refs = refs[:10], refs[10:]
+    stagger, a_theta, a_axial, a_radial, l_rows, r_cols = small[:6]
+    mode_order, mode_radial, mode_plane, gust = small[6:]
+    (
     state,
     source,
     sigma,
@@ -52,7 +48,8 @@
     xrecv_sem,
     psend_sem,
     precv_sem,
-):
+    small_sem,
+    ) = refs
     T, X, H, V, CT, CX, NR, NPASS, NMODE = dims
     F = 2 * V
     CPP = CT // NPASS
@@ -76,12 +73,16 @@
             barrier, inc=1, device_id=(other // X, lax.rem(other, X)), device_id_type=MESH
         )
 
+    little = [
+        pltpu.make_async_copy(src, dst, small_sem.at[i])
+        for i, (src, dst) in enumerate(zip(small_hbm, small))
+    ]
     loads = [
         pltpu.make_async_copy(state_hbm, state.at[:, pl.ds(CX, CT * CX)], load_sem.at[0]),
         pltpu.make_async_copy(sigma_hbm, sigma, load_sem.at[1]),
         pltpu.make_async_copy(source_hbm, source, load_sem.at[2]),
     ]
-    for copy in loads:
+    for copy in loads + little:
         copy.start()
 
     zero = jnp.zeros((H * F, CX, NR), jnp.float32)
@@ -147,6 +148,8 @@
     for h in range(H):
         send(0, h)
 
+    for copy in little:
+        copy.wait()
     loads[1].wait()
     step[...] = courant / (1.0 + sigma[...])
     loads[2].wait()
@@ -171,7 +174,7 @@
                 if factor != 1.0:
                     dt = factor * dt
                 damp = sigma[pl.ds(base, CX)] + 6.0 * viscosity
-                at = [[a_theta[kind, v, w] for w in range(V)] for v in range(V)]
+                at = [[a_theta[v, kind, w] for w in range(V)] for v in range(V)]
                 for p in range(2):
                     flux = [None] * V
                     sums = []
@@ -224,7 +227,7 @@
             for p in range(2):
                 values = [thalo[stage, side, h, p * V + w] for w in range(V)]
                 terms = halo_terms(
-                    values, lambda v, w: a_theta[kind, v, w], -1.0 if side == 0 else 1.0
+                    values, lambda v, w: a_theta[v, kind, w], -1.0 if side == 0 else 1.0
                 )
                 for v in range(V):
                     at = (h * F + p * V + v, pl.ds(offset + t * CX, CX))
@@ -389,6 +392,31 @@
                 x_copy(stage, 1, h).wait_send()
 
 
+def store_kernel(fields, amps, fields_out, amps_out, sems):
+    copies = [
+        pltpu.make_async_copy(fields, fields_out, sems.at[0]),
+        pltpu.make_async_copy(amps, amps_out, sems.at[1]),
+    ]
+    for copy in copies:
+        copy.start()
+    for copy in copies:
+        copy.wait()
+
+
+def store(fields, amps):
+    vmem = pl.BlockSpec(memory_space=pl.ANY)
+    hbm = pl.BlockSpec(memory_space=pltpu.HBM)
+    return pl.pallas_call(
+        store_kernel,
+        out_shape=tuple(jax.ShapeDtypeStruct(a.shape, a.dtype) for a in (fields, amps)),
+        in_specs=(vmem, vmem),
+        out_specs=(hbm, hbm),
+        compiler_params=pltpu.CompilerParams(vmem_limit_bytes=2**20),
+        scratch_shapes=[pltpu.SemaphoreType.DMA((2,))],
+        name="store",
+    )(fields, amps)
+
+
 def local(T, X, *args):
     state, source, sigma, stagger = args[:4]
     H, two, V, CT, CX, NR = state.shape
@@ -400,8 +428,10 @@
     f32 = jnp.float32
     hbm = pl.BlockSpec(memory_space=pl.ANY)
     vmem = pl.BlockSpec(memory_space=pltpu.VMEM)
-    smem = pl.BlockSpec(memory_space=pltpu.SMEM)
     DMA = pltpu.SemaphoreType.DMA
+    stagger, a_theta, a_axial, a_radial, orders, radial, planes, gust, l_rows, r_cols = args[3:]
+    small = [stagger, jnp.swapaxes(a_theta, 0, 1), a_axial, a_radial, l_rows, r_cols]
+    small += [orders, radial, planes, gust]
     pad = -(-2 * H // 8) * 8
     fields, amplitudes = pl.pallas_call(
         functools.partial(kernel, dims),
@@ -409,9 +439,11 @@
             jax.ShapeDtypeStruct((H * F, rows, NR), f32),
             jax.ShapeDtypeStruct((H, 2, 2, NMODE), f32),
         ),
-        in_specs=[hbm, hbm, hbm, smem, smem, smem, smem, vmem, vmem, vmem, vmem, smem, smem],
+        in_specs=[hbm] * 13,
         out_specs=(vmem, vmem),
-        scratch_shapes=[
+        scratch_shapes=[pltpu.SMEM(a.shape, a.dtype) for a in small[:6]]
+        + [pltpu.VMEM(a.shape, a.dtype) for a in small[6:]]
+        + [
             pltpu.VMEM((H * F, rows + 2 * CX, NR), f32),
             pltpu.VMEM((H * F, rows, NR), f32),
             pltpu.VMEM((rows, NR), f32),
@@ -432,17 +464,19 @@
             DMA((2, 2, H)),
             DMA,
             DMA,
+            DMA((10,)),
         ],
         compiler_params=pltpu.CompilerParams(
-            collective_id=0, has_side_effects=True, vmem_limit_bytes=40 * 2**20
+            collective_id=0, has_side_effects=True, vmem_limit_bytes=16 * 2**20
         ),
         name="wake",
     )(
-        state.reshape(H * F, rows, NR),
+        *(pltpu.with_memory_space_constraint(a, pltpu.HBM) for a in (state.reshape(H * F, rows, NR),
         source.reshape(H * F, rows, NR),
         sigma.reshape(rows, NR),
-        *args[3:],
+        *small)),
     )
+    fields, amplitudes = store(fields, amplitudes)
     return fields.reshape(state.shape), amplitudes
 
 

time: 28.5 us -> 22.8 us (0.80)
  local copies, waits for them, and re-layouts: 5.49 us -> 0 us
    unnamed x27 -> x0, local copies, waits for them, and re-layouts: 5.49 us -> none
    pallas_call x0 -> x1, Pallas kernels: none -> 0.97 us  [store(): pl.pallas_call(store_kernel, out_shape=tuple((jax.ShapeDtypeStruct(a.shap...]
    pallas_call x1, Pallas kernels: 21.9 us -> 21.1 us  [local(): pl.pallas_call(functools.partial(kernel, dims), out_shape=(jax.ShapeDtype...]
where the time goes in v2:
time: 22.8 us; the launch traced here: 22.7 us
  Pallas kernels  22 us (96%)
  between operations  0.64 us (3%)
    pallas_call x1, Pallas kernels, local(): pl.pallas_call(functools.partial(kernel, dims), out_shape=(jax.ShapeDtype...  21.1 us
    pallas_call x1, Pallas kernels, store(): pl.pallas_call(store_kernel, out_shape=tuple((jax.ShapeDtypeStruct(a.shap...  0.97 us

profile of v2, /device:TPU:0, one launch (start us, length us, event | category | flops | bytes accessed | tf_op | source)
XLA Modules:
  0.0 22.7 jit_solution(8007134698824173650)
XLA Ops:
  0.6 21.1 %wake.1 = (f32[30,64,128]{2,1,0:T(8,128)S(1)}, f32[3,2,2,128]{3,2,1,0:T(2,128)S(1)}) custom-call(f32[30,64,128]{2,1,0:T(8,128)} %bitcast.5, f32[30,64,128]{2,1,0:T(8,128)} %bitcast.6, f32[64,128]{1,0:T(8,128)} %bitcast.7, s32[2]{0:T(128)} %refs_0_.1, f32[5,4,5]{2,1,0:T(4,128)} %bitcast.8, f32[5,5]{1,0:T(8,128)} %refs_2_.1, f32[5,5]{1,0:T(8,128)} %refs_3_.1, ...), custom_call_target="tpu_custom_call" | custom-call | tf_op jit(solution)/shard_map/wake/pallas_call | solution.py:436
  21.7 1.0 %store.1 = (f32[30,64,128]{2,1,0:T(8,128)}, f32[3,2,2,128]{3,2,1,0:T(2,128)}) custom-call(f32[30,64,128]{2,1,0:T(8,128)S(1)} %get-tuple-element.6.fields, f32[3,2,2,128]{3,2,1,0:T(2,128)S(1)} %get-tuple-element.7.amps), custom_call_target="tpu_custom_call" | custom-call | tf_op jit(solution)/shard_map/store/pallas_call | solution.py:409

commit v3 on v2

--- a/solution.py
+++ b/solution.py
@@ -37,6 +37,7 @@
     xhalo,
     xsend,
     phi,
+    phi_t,
     cosines,
     sines,
     part,
@@ -49,6 +50,12 @@
     psend_sem,
     precv_sem,
     small_sem,
+    kinds,
+    ghost_sigma,
+    ghost_kind,
+    weights,
+    isend_sem,
+    irecv_sem,
     ) = refs
     T, X, H, V, CT, CX, NR, NPASS, NMODE = dims
     F = 2 * V
@@ -66,12 +73,29 @@
 
     barrier = pltpu.get_barrier_semaphore()
 
-    @pl.loop(1, N)
-    def _(i):
-        other = lax.rem(me + i, N)
-        pl.semaphore_signal(
-            barrier, inc=1, device_id=(other // X, lax.rem(other, X)), device_id_type=MESH
-        )
+    def for_others(act):
+        for x in range(X):
+
+            @pl.when(x != xr)
+            def _():
+                act(th, x)
+
+        def ring(j):
+            far = th + j
+            far = jnp.where(far >= T, far - T, far)
+            for x in range(X):
+                act(far, x)
+
+        if T * X <= 64:
+            for j in range(1, T):
+                ring(j)
+        else:
+            pl.loop(1, T)(ring)
+
+    def greet(t, x):
+        pl.semaphore_signal(barrier, inc=1, device_id=(t, x), device_id_type=MESH)
+
+    for_others(greet)
 
     little = [
         pltpu.make_async_copy(src, dst, small_sem.at[i])
@@ -92,12 +116,6 @@
 
     def x_rows(row):
         return pl.ds(row, CT, stride=CX)
-
-    loads[0].wait()
-    for h in range(H):
-        for f in range(F):
-            xsend[0, 0, h, f] = state[h * F + f, x_rows(CX + CX - 1), :]
-            xsend[0, 1, h, f] = state[h * F + f, x_rows(CX), :]
 
     pl.semaphore_wait(barrier, N - 1)
 
@@ -133,9 +151,14 @@
             device_id_type=MESH,
         )
 
-    def send(stage, h):
+    def send_t(stage, h):
         for copy in t_copies(state_hbm if stage == 0 else first, 0 if stage == 0 else CX, stage, h):
             copy.start()
+
+    def send_x(field, stage, h):
+        for f in range(F):
+            xsend[stage, 0, h, f] = field[h * F + f, x_rows(CX + CX - 1), :]
+            xsend[stage, 1, h, f] = field[h * F + f, x_rows(CX), :]
 
         @pl.when(has_hi)
         def _():
@@ -145,11 +168,31 @@
         def _():
             x_copy(stage, 1, h).start()
 
+    def info_copy(what, side):
+        src = sigma_hbm.at[pl.ds((CT - 1) * CX if side == 0 else 0, CX)]
+        return pltpu.make_async_remote_copy(
+            src_ref=src if what == 0 else kinds.at[side],
+            dst_ref=(ghost_sigma if what == 0 else ghost_kind).at[side],
+            send_sem=isend_sem.at[what, side],
+            recv_sem=irecv_sem.at[what, side],
+            device_id=(up if side == 0 else down, xr),
+            device_id_type=MESH,
+        )
+
+    for side in range(2):
+        info_copy(0, side).start()
     for h in range(H):
-        send(0, h)
-
+        send_t(0, h)
     for copy in little:
         copy.wait()
+    for side in range(2):
+        kind = stagger[NPASS - 1 if side == 0 else 0].astype(jnp.float32)
+        kinds[side] = jnp.full((8, NR), kind, jnp.float32)
+        info_copy(1, side).start()
+    loads[0].wait()
+    for h in range(H):
+        send_x(state, 0, h)
+
     loads[1].wait()
     step[...] = courant / (1.0 + sigma[...])
     loads[2].wait()
@@ -218,7 +261,7 @@
             terms.append((sign * 0.5) * total - viscosity * values[v])
         return terms
 
-    def add_halos(result, offset, stage, h, factor):
+    def add_t_halos(result, offset, stage, h, factor):
         for side, copy in enumerate(t_copies(state_hbm, 0, stage, h)):
             copy.wait_recv()
             t = 0 if side == 0 else CT - 1
@@ -232,6 +275,8 @@
                 for v in range(V):
                     at = (h * F + p * V + v, pl.ds(offset + t * CX, CX))
                     result[at] = result[at] - dt * terms[v]
+
+    def add_x_halos(result, offset, stage, h, factor):
         for side in range(2):
 
             @pl.when(has_lo if side == 0 else has_hi)
@@ -251,7 +296,8 @@
 
     main(state, first, CX, 0.5)
 
-    cells = (th * CT + lax.broadcasted_iota(jnp.int32, (CT, NMODE), 0)).astype(jnp.float32)
+    cells = lax.broadcasted_iota(jnp.int32, (2 * CT, NMODE), 0)
+    cells = (th * CT + jnp.where(cells == CT + 1, -1, cells)).astype(jnp.float32)
     radial_pos = lax.broadcasted_iota(jnp.int32, (NR, NMODE), 0).astype(jnp.float32) + 0.5
     for h in range(H):
         turns = mode_order[pl.ds(h, 1)].astype(jnp.float32) * cells
@@ -260,37 +306,109 @@
         cosines[h] = jnp.cos(angle)
         sines[h] = jnp.sin(angle)
         radial = mode_radial[pl.ds(h, 1)]
-        phi[h] = jnp.where(
+        table = jnp.where(
             radial == 0,
             1.0,
             math.sqrt(2.0) * jnp.cos(math.pi * radial.astype(jnp.float32) * radial_pos / NR),
         )
+        phi[h] = table
+        phi_t[h] = table.T
+
+    for what in range(2):
+        for side in range(2):
+            info_copy(what, side).wait_recv()
+
+    def edge_weights(b):
+        x = 0 if b == 0 else CX - 1
+        for side in range(2):
+            dt = courant / (1.0 + ghost_sigma[side, pl.ds(x, 1)])
+            kind = ghost_kind[side, pl.ds(0, 1)]
+            masks = [kind == float(k) for k in range(a_theta.shape[1])]
+            for w in range(V):
+                total = jnp.zeros((1, NR), jnp.float32)
+                for k, mask in enumerate(masks):
+                    row = l_rows[b, 0] * a_theta[0, k, w]
+                    for v in range(1, V):
+                        row = row + l_rows[b, v] * a_theta[v, k, w]
+                    total = jnp.where(mask, row, total)
+                total = (0.5 if side == 0 else -0.5) * total - viscosity * l_rows[b, w]
+                weights[b, side, pl.ds(w, 1)] = -dt * total
+
+    @pl.when(jnp.logical_not(has_lo))
+    def _():
+        edge_weights(0)
+
+    @pl.when(jnp.logical_not(has_hi))
+    def _():
+        edge_weights(1)
 
     for h in range(H):
-        add_halos(first, CX, 0, h, 0.5)
-        for f in range(F):
-            xsend[1, 0, h, f] = first[h * F + f, x_rows(CX + CX - 1), :]
-            xsend[1, 1, h, f] = first[h * F + f, x_rows(CX), :]
-        send(1, h)
-
-    main(first, out, 0, 1.0)
+        add_x_halos(first, CX, 0, h, 0.5)
+        add_t_halos(first, CX, 0, h, 0.5)
+        send_t(1, h)
+        send_x(first, 1, h)
+
+    def plane_value(b, h, p):
+        x = 0 if b == 0 else CX - 1
+        inner = 1 if b == 0 else CX - 2
+        lines = lax.broadcasted_iota(jnp.int32, (CT, NR), 0)
+        freq = base_frequency * (h + 1.0)
+        flux = start = sums = fields = others = forcing = 0.0
+        for w in range(V):
+            f = h * F + p * V + w
+            l = l_rows[b, w]
+            u = first[f, x_rows(CX + x), :]
+            near = first[f, x_rows(CX + inner), :]
+            tm = jnp.where(lines == 0, 0.0, pltpu.roll(u, 1, 0))
+            tp = jnp.where(lines == CT - 1, 0.0, pltpu.roll(u, CT - 1, 0))
+            rm = jnp.where(first_lane, 0.0, pltpu.roll(u, 1, 1))
+            rp = jnp.where(last_lane, 0.0, pltpu.roll(u, NR - 1, 1))
+            gx = gr = 0.0
+            for v in range(V):
+                gx = gx + l_rows[b, v] * a_axial[v, w]
+                gr = gr + l_rows[b, v] * a_radial[v, w]
+            gt = None
+            for k in range(NPASS):
+                row = 0.0
+                for v in range(V):
+                    row = row + l_rows[b, v] * a_theta[v, stagger[k], w]
+                gt = row if gt is None else jnp.where(lines >= k * CPP, row, gt)
+            dx = near if b == 0 else -near
+            flux = flux + (gt * (tp - tm) + gx * dx + gr * (rp - rm))
+            sums = sums + l * ((tp + tm) + near + (rp + rm))
+            fields = fields + l * u
+            others = others + l * first[h * F + (1 - p) * V + w, x_rows(CX + x), :]
+            forcing = forcing + l * source[f, x_rows(x), :]
+            start = start + l * state[f, x_rows(CX + x), :]
+        damp = sigma[x_rows(x), :] + 6.0 * viscosity
+        turned = -freq if p == 0 else freq
+        res = 0.5 * flux - viscosity * sums + damp * fields + turned * others - forcing
+        return start - step[x_rows(x), :] * res
 
     def project(b, h):
         x = 0 if b == 0 else CX - 1
         planes = []
         for p in range(2):
-            total = None
-            for v in range(V):
-                term = l_rows[b, v] * out[h * F + p * V + v, x_rows(x), :]
-                total = term if total is None else total + term
-            planes.append(total)
+            planes.append(plane_value(b, h, p))
+            edges = []
+            for side in range(2):
+                row = CX + x + (0 if side == 0 else (CT - 1) * CX)
+                edge = None
+                for w in range(V):
+                    term = weights[b, side, pl.ds(w, 1)] * first[h * F + p * V + w, pl.ds(row, 1)]
+                    edge = term if edge is None else edge + term
+                edges.append(edge)
+            lines = lax.broadcasted_iota(jnp.int32, (CT, NR), 0)
+            planes.append(
+                jnp.where(lines == 0, edges[1], jnp.where(lines == 1, edges[0], 0.0))
+            )
         projected = jnp.dot(
             jnp.concatenate(planes, axis=0),
             phi[h],
             precision=highest,
             preferred_element_type=jnp.float32,
         )
-        real, imag = projected[:CT], projected[CT:]
+        real, imag = projected[: 2 * CT], projected[2 * CT :]
         weight = jnp.where(mode_plane[pl.ds(h, 1)] == b, scale, 0.0)
         part_real = jnp.sum(real * cosines[h] + imag * sines[h], axis=0, keepdims=True)
         part_imag = jnp.sum(imag * cosines[h] - real * sines[h], axis=0, keepdims=True)
@@ -299,7 +417,6 @@
 
     part[...] = jnp.zeros_like(part)
     for h in range(H):
-        add_halos(out, 0, 1, h, 1.0)
 
         @pl.when(jnp.logical_not(has_lo))
         def _():
@@ -309,21 +426,23 @@
         def _():
             project(1, h)
 
-    def part_copy(other):
-        return pltpu.make_async_remote_copy(
+    def share(t, x):
+        copy = pltpu.make_async_remote_copy(
             src_ref=part,
             dst_ref=parts.at[me],
             send_sem=psend_sem,
             recv_sem=precv_sem,
-            device_id=(other // X, lax.rem(other, X)),
+            device_id=(t, x),
             device_id_type=MESH,
         )
-
-    @pl.loop(1, N)
-    def _(i):
-        part_copy(lax.rem(me + i, N)).start()
-
+        copy.start()
+
+    for_others(share)
     parts[me] = part[...]
+    main(first, out, 0, 1.0)
+    for h in range(H):
+        add_t_halos(out, 0, 1, h, 1.0)
+        add_x_halos(out, 0, 1, h, 1.0)
     everyone = pltpu.make_async_remote_copy(
         src_ref=parts.at[pl.ds(0, N - 1)],
         dst_ref=parts.at[pl.ds(0, N - 1)],
@@ -351,13 +470,13 @@
         weight = jnp.where(mode_plane[pl.ds(h, 1)] == b, scale, 0.0)
         real = weight * (part_rows[2 * h] - gust[h, pl.ds(0, 1)])
         imag = weight * (part_rows[2 * h + 1] - gust[h, pl.ds(1, 1)])
+        cos, sin = cosines[h, pl.ds(0, CT)], sines[h, pl.ds(0, CT)]
         coef = jnp.concatenate(
-            [real * cosines[h] - imag * sines[h], real * sines[h] + imag * cosines[h]], axis=0
+            [real * cos - imag * sin, real * sin + imag * cos], axis=0
         )
-        q = lax.dot_general(
+        q = jnp.dot(
             coef,
-            phi[h],
-            (((1,), (1,)), ((), ())),
+            phi_t[h],
             precision=highest,
             preferred_element_type=jnp.float32,
         )
@@ -377,6 +496,9 @@
             correct(1, h)
 
     everyone.wait_send()
+    for what in range(2):
+        for side in range(2):
+            info_copy(what, side).wait_send()
     for stage in range(2):
         for h in range(H):
             src = state_hbm if stage == 0 else first
@@ -453,8 +575,9 @@
             pltpu.VMEM((2, 2, H, F, CT, NR), f32),
             pltpu.VMEM((2, 2, H, F, CT, NR), f32),
             pltpu.VMEM((H, NR, NMODE), f32),
-            pltpu.VMEM((H, CT, NMODE), f32),
-            pltpu.VMEM((H, CT, NMODE), f32),
+            pltpu.VMEM((H, NMODE, NR), f32),
+            pltpu.VMEM((H, 2 * CT, NMODE), f32),
+            pltpu.VMEM((H, 2 * CT, NMODE), f32),
             pltpu.VMEM((pad, NMODE), f32),
             pltpu.VMEM((N, pad, NMODE), f32),
             DMA((3,)),
@@ -465,6 +588,12 @@
             DMA,
             DMA,
             DMA((10,)),
+            pltpu.VMEM((2, 8, NR), f32),
+            pltpu.VMEM((2, CX, NR), f32),
+            pltpu.VMEM((2, 8, NR), f32),
+            pltpu.VMEM((2, 2, V, NR), f32),
+            DMA((2, 2)),
+            DMA((2, 2)),
         ],
         compiler_params=pltpu.CompilerParams(
             collective_id=0, has_side_effects=True, vmem_limit_bytes=16 * 2**20

time: 22.8 us -> 21.5 us (0.943)
  Pallas kernels: 22 us -> 20.7 us
    pallas_call x1, Pallas kernels: 21.1 us -> 19.7 us  [local(): pl.pallas_call(functools.partial(kernel, dims), out_shape=(jax.ShapeDtype...]
where the time goes in v3:
time: 21.5 us; the launch traced here: 21.3 us
  Pallas kernels  20.7 us (96%)
  between operations  0.64 us (3%)
    pallas_call x1, Pallas kernels, local(): pl.pallas_call(functools.partial(kernel, dims), out_shape=(jax.ShapeDtype...  19.7 us
    pallas_call x1, Pallas kernels, store(): pl.pallas_call(store_kernel, out_shape=tuple((jax.ShapeDtypeStruct(a.shap...  0.97 us

profile of v3, /device:TPU:0, one launch (start us, length us, event | category | flops | bytes accessed | tf_op | source)
XLA Modules:
  0.0 21.3 jit_solution(6194448219923165181)
XLA Ops:
  0.6 19.7 %wake.1 = (f32[30,64,128]{2,1,0:T(8,128)S(1)}, f32[3,2,2,128]{3,2,1,0:T(2,128)S(1)}) custom-call(f32[30,64,128]{2,1,0:T(8,128)} %bitcast.5, f32[30,64,128]{2,1,0:T(8,128)} %bitcast.6, f32[64,128]{1,0:T(8,128)} %bitcast.7, s32[2]{0:T(128)} %refs_0_.1, f32[5,4,5]{2,1,0:T(4,128)} %bitcast.8, f32[5,5]{1,0:T(8,128)} %refs_2_.1, f32[5,5]{1,0:T(8,128)} %refs_3_.1, ...), custom_call_target="tpu_custom_call" | custom-call | tf_op jit(solution)/shard_map/wake/pallas_call | solution.py:558
  20.4 1.0 %store.1 = (f32[30,64,128]{2,1,0:T(8,128)}, f32[3,2,2,128]{3,2,1,0:T(2,128)}) custom-call(f32[30,64,128]{2,1,0:T(8,128)S(1)} %get-tuple-element.6.fields, f32[3,2,2,128]{3,2,1,0:T(2,128)S(1)} %get-tuple-element.7.amps), custom_call_target="tpu_custom_call" | custom-call | tf_op jit(solution)/shard_map/store/pallas_call | solution.py:531
